TPU v7x, 512 devices: a whole 4x4x16 slice. The times are simulated.
512 devices in a mesh: wa: 4 (over x), vert: 128 (over y, z, core).
Axes of the slice: x: 4, y: 4, z: 16, core: 2. Of those that a mesh axis runs over, the one named last changes fastest.
Arguments:
- hidden: bfloat16 [16384, 1024], P('vert', 'wa'), as said below
- norm_gain: bfloat16 [1024], P('wa'), may hold values from 0.5 to 1.5
- head_weight: bfloat16 [1024, 32128], P('wa', 'vert'), as said below
- target_ids: int32 [16384], P('vert'), may hold values from 0 to 32127
- seq_lengths: int32 [65], replicated, may hold values from 1 to 8192, as said below
Outputs:
- token_logprob: float32 [16384], P('vert')
- token_entropy: float32 [16384], P('vert')
Inputs may be any that keep to these rules, and one draw needn't show every extreme that they name: `seq_lengths`: entry 0 equals 8192; every other entry lies between 1 and 128, and at least one of them equals 128. `hidden`: hidden states of any scale per slot; the norm removes it. `head_weight`: entries of order 3 / sqrt(1024) times a per-column scale.
All inputs are finite; a program needn't handle non-finite values.
Results may differ from a plain program's by a relative error of at most 0.012.
The roundings to bfloat16 on the way count: a program that leaves them out, or rounds other values in their place, can miss the bound.
Values may be sent and summed in bfloat16 or wider, within the bound.
A program may use at most 64 MiB of HBM per device.

v0:
```python
import jax
import jax.numpy as jnp
from jax import lax
from jax.sharding import Mesh
from jax.sharding import PartitionSpec as P

D = 1024
SHORT = 128
norm_epsilon = 1e-06
VERT = ("y", "z", "c")
TOKEN_AXES = ("z", "c")


def live_mask(positions, seq_lengths, long_len, short_len):
    is_long = positions < long_len
    beyond = jnp.maximum(positions - long_len, 0)
    seq_index = jnp.where(is_long, 0, 1 + beyond // short_len)
    offset = jnp.where(is_long, positions, beyond % short_len)
    return offset < jnp.take(seq_lengths, seq_index)


def per_device(hidden, norm_gain, head_weight, target_ids, seq_lengths):
    x_count = lax.axis_size("x")
    y_count = lax.axis_size("y")
    z_count = lax.axis_size("z")
    c_count = lax.axis_size("c")
    x_index = lax.axis_index("x")
    y_index = lax.axis_index("y")
    z_index = lax.axis_index("z")
    c_index = lax.axis_index("c")
    vert_count = y_count * z_count * c_count
    vert_index = (y_index * z_count + z_index) * c_count + c_index
    tok_local = hidden.shape[0]
    quarter = tok_local // x_count
    vocab_local = head_weight.shape[1]
    group_count = z_count * c_count
    rows = lax.all_to_all(hidden, "x", split_axis=0, concat_axis=1, tiled=True)
    gain_full = lax.all_gather(norm_gain, "x", axis=0, tiled=True)
    values = rows.astype(jnp.float32)
    squares = jnp.sum(values * values, axis=1, keepdims=True)
    normed = (
        values * lax.rsqrt(squares / D + norm_epsilon) * gain_full.astype(jnp.float32)
    ).astype(jnp.bfloat16)
    group_rows = lax.all_gather(normed, TOKEN_AXES, axis=0, tiled=True)
    group_ids = lax.all_gather(target_ids, TOKEN_AXES, axis=0)
    group_ids = lax.dynamic_slice_in_dim(group_ids, x_index * quarter, quarter, 1).reshape(-1)
    weight = lax.all_gather(head_weight, ("x", "y"), axis=0)
    weight = weight.reshape(x_count, y_count, D // x_count, vocab_local)
    logits = jnp.einsum(
        "txd,xyde->tye",
        group_rows.reshape(-1, x_count, D // x_count),
        weight,
        preferred_element_type=jnp.float32,
    )
    block_of = (
        lax.broadcasted_iota(jnp.int32, (1, y_count, vocab_local), 1) * z_count + z_index
    ) * c_count + c_index
    column_ids = block_of * vocab_local + lax.broadcasted_iota(
        jnp.int32, (1, y_count, vocab_local), 2
    )
    row_peak = jnp.max(logits, axis=(1, 2))
    scaled = jnp.exp(logits - row_peak[:, None, None])
    row_sum = jnp.sum(scaled, axis=(1, 2))
    row_weighted = jnp.sum(scaled * logits, axis=(1, 2))
    row_picked = jnp.sum(
        jnp.where(column_ids == group_ids[:, None, None], logits, 0.0), axis=(1, 2)
    )
    stats = jnp.stack([row_peak, row_sum, row_weighted, row_picked]).reshape(
        4, group_count, quarter
    )
    parts = lax.all_to_all(stats, TOKEN_AXES, split_axis=1, concat_axis=1, tiled=True)
    part_peak, part_sum, part_weighted, part_picked = (parts[0], parts[1], parts[2], parts[3])
    highest = jnp.max(part_peak, axis=0)
    factor = jnp.exp(part_peak - highest[None, :])
    totals = jnp.sum(part_sum * factor, axis=0)
    weighted = jnp.sum(part_weighted * factor, axis=0)
    picked = jnp.sum(part_picked, axis=0)
    log_norm = highest + jnp.log(totals)
    logprob = picked - log_norm
    entropy = log_norm - weighted / totals
    full_logprob, full_entropy = (
        lax.all_gather(logprob, "x", axis=0, tiled=True),
        lax.all_gather(entropy, "x", axis=0, tiled=True),
    )
    positions = vert_index * tok_local + jnp.arange(tok_local, dtype=jnp.int32)
    live_rows = live_mask(positions, seq_lengths, vert_count * tok_local // 2, SHORT)
    return (jnp.where(live_rows, full_logprob, 0.0), jnp.where(live_rows, full_entropy, 0.0))


def solution(mesh):
    wa_count, vert_count = mesh.devices.shape
    y_count = 4
    c_count = 2
    z_count = vert_count // (y_count * c_count)
    fine = Mesh(mesh.devices.reshape(wa_count, y_count, z_count, c_count), ("x",) + VERT)
    in_specs = (P(VERT, "x"), P("x"), P("x", VERT), P(VERT), P())
    out_specs = (P(VERT), P(VERT))
    return jax.shard_map(
        per_device, mesh=fine, in_specs=in_specs, out_specs=out_specs, check_vma=False
    )
```

profile of v0, /device:TPU:32, one launch (start us, length us, event | category | flops | bytes accessed | tf_op | source)
XLA Modules:
  0.0 210.9 jit_solution(2471399766707559232)
XLA Ops:
  7.2 0.0 copy-start
  7.2 4.3 %all-to-all-start = ((bf16[4,32,256]{2,1,0:T(8,128)(2,1)}), bf16[4,32,256]{2,1,0:T(8,128)(2,1)S(1)}, u32[]{:S(2)}, u32[]{:S(2)}) async-start(bf16[4,32,256]{2,1,0:T(8,128)(2,1)} %bitcast.53), calls=%async_computation | async-start | bytes 131072 | tf_op jit(solution)/shard_map/all_to_all | solution.py:37
  11.5 0.0 all-gather.7.cloned.1.call-start
  11.5 0.7 reshape.134
  12.1 10.2 %all-gather.2 = bf16[4,1,256]{2,1,0:T(2,128)(2,1)S(1)} all-gather(bf16[1,1,256]{2,1,0:T(2,128)(2,1)S(1)} %reshape.134), channel_id=1, replica_groups=mesh['x'=4,'y'=4,'z'=16,'c'=2] {'x'}, dimensions={0}, use_global_device_ids=true | all-gather | bytes 2560 | tf_op jit(solution)/shard_map/all_gather | solution.py:38
  22.3 0.0 all-to-all-done
  22.4 0.1 fusion.4
  22.5 0.7 multiply_convert_fusion
  23.2 0.0 all-gather.7.cloned.1.call-update
  23.2 0.0 all-gather.9.cloned.1.call-start
  23.3 0.7 all-gather.9.cloned.1.call-update
  24.0 34.1 %all-gather.3 = s32[32,1,128]{2,1,0:T(1,128)S(1)} all-gather(s32[1,1,128]{2,1,0:T(1,128)} %bitcast.55), channel_id=3, replica_groups=mesh['x'=4,'y'=4,'z'=16,'c'=2] {'z','c'}, dimensions={0}, use_global_device_ids=true | all-gather | bytes 16896 | tf_op jit(solution)/shard_map/all_gather | solution.py:45
  58.1 0.1 dynamic-slice_reduce_fusion
  58.2 0.1 eq.18
  58.3 1.3 dynamic-slice
  60.2 0.1 iota_add_fusion
  60.3 36.7 %all-gather.7.cloned.1.call-done = bf16[1024,1024]{1,0:T(8,128)(2,1)} async-done(((bf16[32,1024]{1,0:T(8,128)(2,1)}), bf16[1024,1024]{1,0:T(8,128)(2,1)}) %all-gather.7.cloned.1.call-update) | async-done | bytes 2097168 | tf_op jit(solution)/shard_map/all_gather | solution.py:44
  97.0 2.9 %copy.12 = bf16[1024,1024]{0,1:T(8,128)(2,1)S(1)} copy(bf16[1024,1024]{1,0:T(8,128)(2,1)} %all-gather.7.cloned.1.call-done) | data formatting | bytes 4194304 | tf_op jit(solution)/shard_map/all_gather | solution.py:44
  99.9 57.4 %all-gather.9.cloned.1.call-done = bf16[4096,251]{1,0:T(8,128)(2,1)} async-done(((bf16[256,251]{1,0:T(8,128)(2,1)}), bf16[4096,251]{1,0:T(8,128)(2,1)}) %all-gather.9.cloned.1.call-update) | async-done | bytes 2056208 | tf_op jit(solution)/shard_map/all_gather | solution.py:47
  157.3 5.9 %bitcast_reduce_fusion = (f32[1024]{0:T(1024)S(1)}, f32[1024,4,251,1]{0,2,1,3:T(8,128)}) fusion(bf16[1024,4,256,1]{0,2,3,1:T(8,128)(2,1)S(1)} %bitcast.46, bf16[4,4,256,251]{3,2,1,0:T(8,128)(2,1)} %bitcast.56), kind=kOutput, calls=%fused_computation.4 | convolution fusion | flops 2106567680 | bytes 8269824 | tf_op jit(solution)/shard_map/txd,xyde->tye/dot_general | solution.py:49
  163.2 0.1 stack.15
  163.3 2.9 %fusion.1 = (f32[1024]{0:T(1024)S(1)}, f32[1024]{0:T(1024)S(1)}, f32[1024]{0:T(1024)S(1)}) fusion(f32[1024,4,251,1]{0,2,1,3:T(8,128)} %get-tuple-element.16, f32[1024]{0:T(1024)S(1)} %get-tuple-element.15, s32[1024]{0:T(1024)S(1)} %eq.18, s32[4,251]{1,0:T(4,128)S(1)} %iota_add_fusion), kind=kLoop, calls=%fused_computation.6 | loop fusion | flops 7193600 | bytes 4136880 | tf_op jit(solution)/shard_map/reduce_sum | solution.py:63
  166.2 0.1 stack.18
  166.3 0.1 stack.17
  166.4 0.1 stack.16
  166.5 0.1 fusion.9
  166.6 0.7 reshape.155
  167.3 12.8 %all-to-all-start.1 = ((f32[32,1,128]{2,1,0:T(1,128)}), f32[32,1,128]{2,1,0:T(1,128)S(1)}, u32[]{:S(2)}, u32[]{:S(2)}) async-start(f32[32,1,128]{2,1,0:T(1,128)} %reshape.155), calls=%async_computation.1 | async-start | bytes 32768 | tf_op jit(solution)/shard_map/all_to_all | solution.py:71
  180.1 0.0 copy-done
  180.1 1.2 gather_fusion
  181.4 9.9 %all-to-all-done.1 = f32[32,1,128]{2,1,0:T(1,128)S(1)} async-done(((f32[32,1,128]{2,1,0:T(1,128)}), f32[32,1,128]{2,1,0:T(1,128)S(1)}, u32[]{:S(2)}, u32[]{:S(2)}) %all-to-all-start.1) | async-done | bytes 16416 | tf_op jit(solution)/shard_map/all_to_all | solution.py:71
  191.3 0.5 broadcast.223
  191.8 0.7 reduce.8
  192.5 0.1 reshape.156
  192.6 0.1 fusion.8
  192.7 0.1 subtract_dynamic-update-slice_fusion.1
  192.8 0.1 subtract_dynamic-update-slice_fusion
  192.9 10.1 %all-reduce.2 = (f32[128]{0:T(128)S(1)}, f32[128]{0:T(128)S(1)}) all-reduce(f32[128]{0:T(128)S(1)} %subtract_dynamic-update-slice_fusion.1, f32[128]{0:T(128)S(1)} %subtract_dynamic-update-slice_fusion), channel_id=1, replica_groups=mesh['x'=4,'y'=4,'z'=16,'c'=2] {'x'}, use_global_device_ids=true, to_apply=%add | all-reduce | flops 256 | bytes 2048
  203.0 0.5 broadcast_select_fusion
  203.5 0.5 broadcast_select_fusion.1
  (11 shorter events, 0.1 us)
Async XLA Ops:
  7.2 173.0 %copy-start = (s32[65]{0:T(128)S(1)}, s32[65]{0:T(128)}, u32[]{:S(2)}) copy-start(s32[65]{0:T(128)} %param.9) | copy-start | bytes 784
  7.2 15.2 %all-to-all-start = ((bf16[4,32,256]{2,1,0:T(8,128)(2,1)}), bf16[4,32,256]{2,1,0:T(8,128)(2,1)S(1)}, u32[]{:S(2)}, u32[]{:S(2)}) async-start(bf16[4,32,256]{2,1,0:T(8,128)(2,1)} %bitcast.53), calls=%async_computation | async-start | bytes 131072 | tf_op jit(solution)/shard_map/all_to_all | solution.py:37
  11.5 85.6 %all-gather.7.cloned.1.call-start = ((), (), s32[]{:S(2)}) async-start(), calls=%async_computation.2 | async-start | bytes 2162688 | tf_op jit(solution)/shard_map/all_gather | solution.py:44
  23.2 134.1 %all-gather.9.cloned.1.call-start = ((), (), s32[]{:S(2)}) async-start(), calls=%async_computation.3 | async-start | bytes 2228224 | tf_op jit(solution)/shard_map/all_gather | solution.py:47
  167.3 24.0 %all-to-all-start.1 = ((f32[32,1,128]{2,1,0:T(1,128)}), f32[32,1,128]{2,1,0:T(1,128)S(1)}, u32[]{:S(2)}, u32[]{:S(2)}) async-start(f32[32,1,128]{2,1,0:T(1,128)} %reshape.155), calls=%async_computation.1 | async-start | bytes 32768 | tf_op jit(solution)/shard_map/all_to_all | solution.py:71
Sparse Core Ops, SparseCore 0:
  23.4 73.6 all-gather.6
  100.1 57.2 all-gather.8
where the time goes:
time: 211 us
  waiting for transfers between devices  105 us (50%)
  blocking collectives  54.3 us (26%)
  starting transfers between devices  17.2 us (8%)
  between operations  14.8 us (7%)
  local copies, waits for them, and re-layouts  7.86 us (4%)
  other arithmetic  6.01 us (3%)
  matrix products  5.9 us (3%)
    all_gather x1, waiting for transfers between devices, per_device(): weight = lax.all_gather(head_weight, ('x', 'y'), axis=0)  57.4 us
    all_gather x1, waiting for transfers between devices, per_device(): group_rows = lax.all_gather(normed, TOKEN_AXES, axis=0, tiled=True)  36.7 us
    all_gather x1, blocking collectives, per_device(): group_ids = lax.all_gather(target_ids, TOKEN_AXES, axis=0)  34.1 us
    all_to_all x1, starting transfers between devices, per_device(): lax.all_to_all(stats, TOKEN_AXES, split_axis=1, concat_axis=1, tiled=True)  12.8 us
    all_gather x1, blocking collectives, per_device(): gain_full = lax.all_gather(norm_gain, 'x', axis=0, tiled=True)  10.2 us
    unnamed x1, blocking collectives  10.1 us
    all_to_all x1, waiting for transfers between devices, per_device(): lax.all_to_all(stats, TOKEN_AXES, split_axis=1, concat_axis=1, tiled=True)  9.93 us
    dot_general x1, matrix products, per_device(): jnp.einsum('txd,xyde->tye', group_rows.reshape(-1, x_count, D // x_count)...  5.9 us
  transfers between devices with their start and end apart: 4, of which 3 were waited for; matrix products, arithmetic and copies ran while one was open for 3% of the time, Pallas kernels for 0%

commit v1 on v0

--- a/solution.py
+++ b/solution.py
@@ -35,7 +35,9 @@
     vocab_local = head_weight.shape[1]
     group_count = z_count * c_count
     rows = lax.all_to_all(hidden, "x", split_axis=0, concat_axis=1, tiled=True)
-    gain_full = lax.all_gather(norm_gain, "x", axis=0, tiled=True)
+    gain_full = jnp.concatenate(
+        lax.all_to_all(jnp.stack([norm_gain] * lax.axis_size("x")), "x", 0, 0), axis=0
+    )
     values = rows.astype(jnp.float32)
     squares = jnp.sum(values * values, axis=1, keepdims=True)
     normed = (

time: 211 us -> 217 us (1.028)
  waiting for transfers between devices: 105 us -> 111 us
    all_gather x1 -> x0, blocking collectives: 10.2 us -> none  [per_device(): gain_full = lax.all_gather(norm_gain, 'x', axis=0, tiled=True)]
    all_to_all x0 -> x1, blocking collectives: none -> 9.35 us  [per_device(): lax.all_to_all(jnp.stack([norm_gain] * lax.axis_size('x')), 'x', 0, 0)]
    all_to_all x1, waiting for transfers between devices: 0.01 us -> 5.51 us  [per_device(): rows = lax.all_to_all(hidden, 'x', split_axis=0, concat_axis=1, tiled=True)]
  transfers between devices with their start and end apart: 4 -> 4, of which waited for: 3 -> 4; matrix products, arithmetic and copies ran while one was open for 3% -> 3% of each run, Pallas kernels for 0% -> 0%
where the time goes in v1:
time: 217 us; the launch traced here: 216 us
  waiting for transfers between devices  111 us (51%)
  blocking collectives  53.5 us (25%)
  starting transfers between devices  16.2 us (7%)
  between operations  14.8 us (7%)
  local copies, waits for them, and re-layouts  8.41 us (4%)
  other arithmetic  6.68 us (3%)
  matrix products  5.9 us (3%)
    all_gather x1, waiting for transfers between devices, per_device(): weight = lax.all_gather(head_weight, ('x', 'y'), axis=0)  57.4 us
    all_gather x1, waiting for transfers between devices, per_device(): group_rows = lax.all_gather(normed, TOKEN_AXES, axis=0, tiled=True)  37.1 us
    all_gather x1, blocking collectives, per_device(): group_ids = lax.all_gather(target_ids, TOKEN_AXES, axis=0)  34.1 us
    all_to_all x1, starting transfers between devices, per_device(): lax.all_to_all(stats, TOKEN_AXES, split_axis=1, concat_axis=1, tiled=True)  12.8 us
    unnamed x1, blocking collectives  10.1 us
    all_to_all x1, waiting for transfers between devices, per_device(): lax.all_to_all(stats, TOKEN_AXES, split_axis=1, concat_axis=1, tiled=True)  9.93 us
    all_to_all x1, blocking collectives, per_device(): lax.all_to_all(jnp.stack([norm_gain] * lax.axis_size('x')), 'x', 0, 0)  9.35 us
    dot_general x1, matrix products, per_device(): jnp.einsum('txd,xyde->tye', group_rows.reshape(-1, x_count, D // x_count)...  5.9 us
  transfers between devices with their start and end apart: 4, of which 4 were waited for; matrix products, arithmetic and copies ran while one was open for 3% of the time, Pallas kernels for 0%

profile of v1, /device:TPU:32, one launch (start us, length us, event | category | flops | bytes accessed | tf_op | source)
XLA Modules:
  0.0 216.1 jit_solution(3382895561378717201)
XLA Ops:
  7.2 0.0 copy-start
  7.2 0.7 stack.22
  7.8 0.5 broadcast.226
  8.4 0.7 reduce.8
  9.0 9.3 %all_to_all.24 = bf16[4,2,128]{2,1,0:T(2,128)(2,1)S(1)} all-to-all(bf16[4,2,128]{2,1,0:T(2,128)(2,1)S(1)} %reshape.168), channel_id=1, replica_groups=mesh['x'=4,'y'=4,'z'=16,'c'=2] {'x'}, dimensions={0} | all-to-all | bytes 4096 | tf_op jit(solution)/shard_map/all_to_all | solution.py:39
  18.4 3.3 %all-to-all-start = ((bf16[4,32,256]{2,1,0:T(8,128)(2,1)}), bf16[4,32,256]{2,1,0:T(8,128)(2,1)S(1)}, u32[]{:S(2)}, u32[]{:S(2)}) async-start(bf16[4,32,256]{2,1,0:T(8,128)(2,1)} %bitcast.53), calls=%async_computation | async-start | bytes 131072 | tf_op jit(solution)/shard_map/all_to_all | solution.py:37
  21.7 0.0 all-gather.6.cloned.1.call-start
  21.8 5.5 %all-to-all-done = bf16[4,32,256]{2,1,0:T(8,128)(2,1)S(1)} async-done(((bf16[4,32,256]{2,1,0:T(8,128)(2,1)}), bf16[4,32,256]{2,1,0:T(8,128)(2,1)S(1)}, u32[]{:S(2)}, u32[]{:S(2)}) %all-to-all-start) | async-done | bytes 65568 | tf_op jit(solution)/shard_map/all_to_all | solution.py:37
  27.3 0.1 fusion.4
  27.4 0.7 multiply_convert_fusion
  28.1 0.0 all-gather.6.cloned.1.call-update
  28.2 0.0 all-gather.8.cloned.1.call-start
  28.2 0.7 all-gather.8.cloned.1.call-update
  28.9 34.1 %all-gather.2 = s32[32,1,128]{2,1,0:T(1,128)S(1)} all-gather(s32[1,1,128]{2,1,0:T(1,128)} %bitcast.55), channel_id=3, replica_groups=mesh['x'=4,'y'=4,'z'=16,'c'=2] {'z','c'}, dimensions={0}, use_global_device_ids=true | all-gather | bytes 16896 | tf_op jit(solution)/shard_map/all_gather | solution.py:47
  63.0 0.1 dynamic-slice_reduce_fusion
  63.1 0.1 eq.18
  63.2 1.3 dynamic-slice
  65.2 0.1 iota_add_fusion
  65.2 37.1 %all-gather.6.cloned.1.call-done = bf16[1024,1024]{1,0:T(8,128)(2,1)} async-done(((bf16[32,1024]{1,0:T(8,128)(2,1)}), bf16[1024,1024]{1,0:T(8,128)(2,1)}) %all-gather.6.cloned.1.call-update) | async-done | bytes 2097168 | tf_op jit(solution)/shard_map/all_gather | solution.py:46
  102.3 2.9 %copy.12 = bf16[1024,1024]{0,1:T(8,128)(2,1)S(1)} copy(bf16[1024,1024]{1,0:T(8,128)(2,1)} %all-gather.6.cloned.1.call-done) | data formatting | bytes 4194304 | tf_op jit(solution)/shard_map/all_gather | solution.py:46
  105.2 57.4 %all-gather.8.cloned.1.call-done = bf16[4096,251]{1,0:T(8,128)(2,1)} async-done(((bf16[256,251]{1,0:T(8,128)(2,1)}), bf16[4096,251]{1,0:T(8,128)(2,1)}) %all-gather.8.cloned.1.call-update) | async-done | bytes 2056208 | tf_op jit(solution)/shard_map/all_gather | solution.py:49
  162.6 5.9 %bitcast_reduce_fusion = (f32[1024]{0:T(1024)S(1)}, f32[1024,4,251,1]{0,2,1,3:T(8,128)}) fusion(bf16[1024,4,256,1]{0,2,3,1:T(8,128)(2,1)S(1)} %bitcast.46, bf16[4,4,256,251]{3,2,1,0:T(8,128)(2,1)} %bitcast.56), kind=kOutput, calls=%fused_computation.4 | convolution fusion | flops 2106567680 | bytes 8269824 | tf_op jit(solution)/shard_map/txd,xyde->tye/dot_general | solution.py:51
  168.5 0.1 stack.23
  168.5 2.9 %fusion.1 = (f32[1024]{0:T(1024)S(1)}, f32[1024]{0:T(1024)S(1)}, f32[1024]{0:T(1024)S(1)}) fusion(f32[1024,4,251,1]{0,2,1,3:T(8,128)} %get-tuple-element.16, f32[1024]{0:T(1024)S(1)} %get-tuple-element.15, s32[1024]{0:T(1024)S(1)} %eq.18, s32[4,251]{1,0:T(4,128)S(1)} %iota_add_fusion), kind=kLoop, calls=%fused_computation.6 | loop fusion | flops 7193600 | bytes 4136880 | tf_op jit(solution)/shard_map/reduce_sum | solution.py:65
  171.5 0.1 stack.26
  171.6 0.1 stack.25
  171.7 0.1 stack.24
  171.7 0.1 fusion.9
  171.8 0.7 reshape.170
  172.5 12.8 %all-to-all-start.2 = ((f32[32,1,128]{2,1,0:T(1,128)}), f32[32,1,128]{2,1,0:T(1,128)S(1)}, u32[]{:S(2)}, u32[]{:S(2)}) async-start(f32[32,1,128]{2,1,0:T(1,128)} %reshape.170), calls=%async_computation.2 | async-start | bytes 32768 | tf_op jit(solution)/shard_map/all_to_all | solution.py:73
  185.4 0.0 copy-done
  185.4 1.2 gather_fusion
  186.6 9.9 %all-to-all-done.2 = f32[32,1,128]{2,1,0:T(1,128)S(1)} async-done(((f32[32,1,128]{2,1,0:T(1,128)}), f32[32,1,128]{2,1,0:T(1,128)S(1)}, u32[]{:S(2)}, u32[]{:S(2)}) %all-to-all-start.2) | async-done | bytes 16416 | tf_op jit(solution)/shard_map/all_to_all | solution.py:73
  196.5 0.5 broadcast.227
  197.0 0.7 reduce.9
  197.7 0.1 reshape.171
  197.8 0.1 fusion.8
  198.0 0.1 subtract_dynamic-update-slice_fusion.1
  198.1 0.1 subtract_dynamic-update-slice_fusion
  198.2 10.1 %all-reduce.2 = (f32[128]{0:T(128)S(1)}, f32[128]{0:T(128)S(1)}) all-reduce(f32[128]{0:T(128)S(1)} %subtract_dynamic-update-slice_fusion.1, f32[128]{0:T(128)S(1)} %subtract_dynamic-update-slice_fusion), channel_id=1, replica_groups=mesh['x'=4,'y'=4,'z'=16,'c'=2] {'x'}, use_global_device_ids=true, to_apply=%add | all-reduce | flops 256 | bytes 2048
  208.2 0.5 broadcast_select_fusion
  208.8 0.5 broadcast_select_fusion.1
  (13 shorter events, 0.1 us)
Async XLA Ops:
  7.2 178.2 %copy-start = (s32[65]{0:T(128)S(1)}, s32[65]{0:T(128)}, u32[]{:S(2)}) copy-start(s32[65]{0:T(128)} %param.9) | copy-start | bytes 784
  18.4 8.9 %all-to-all-start = ((bf16[4,32,256]{2,1,0:T(8,128)(2,1)}), bf16[4,32,256]{2,1,0:T(8,128)(2,1)S(1)}, u32[]{:S(2)}, u32[]{:S(2)}) async-start(bf16[4,32,256]{2,1,0:T(8,128)(2,1)} %bitcast.53), calls=%async_computation | async-start | bytes 131072 | tf_op jit(solution)/shard_map/all_to_all | solution.py:37
  21.7 80.6 %all-gather.6.cloned.1.call-start = ((), (), s32[]{:S(2)}) async-start(), calls=%async_computation.3 | async-start | bytes 2162688 | tf_op jit(solution)/shard_map/all_gather | solution.py:46
  28.2 134.4 %all-gather.8.cloned.1.call-start = ((), (), s32[]{:S(2)}) async-start(), calls=%async_computation.4 | async-start | bytes 2228224 | tf_op jit(solution)/shard_map/all_gather | solution.py:49
  172.5 24.0 %all-to-all-start.2 = ((f32[32,1,128]{2,1,0:T(1,128)}), f32[32,1,128]{2,1,0:T(1,128)S(1)}, u32[]{:S(2)}, u32[]{:S(2)}) async-start(f32[32,1,128]{2,1,0:T(1,128)} %reshape.170), calls=%async_computation.2 | async-start | bytes 32768 | tf_op jit(solution)/shard_map/all_to_all | solution.py:73
Sparse Core Ops, SparseCore 0:
  28.3 73.9 all-gather.5
  105.3 57.1 all-gather.7
